TPU v7x, 32 devices: a whole 2x2x4 slice. The times are simulated.
32 devices in a mesh: row: 4 (over z), col: 8 (over y, x, core).
Axes of the slice: x: 2, y: 2, z: 4, core: 2. Of those that a mesh axis runs over, the one named last changes fastest.
Arguments:
- block_cells: float32 [352, 5, 16, 256], P(('row', 'col')), may hold values from -0.6 to 1.4, as said below
- slot_blocks: int32 [32, 11], replicated, may hold values from -1 to 191, as said below
Outputs:
- new_cells: float32 [224, 5, 16, 256], P(('row', 'col'))
Inputs may be any that keep to these rules, and one draw needn't show every extreme that they name: `slot_blocks`: row r * 8 + c lists the blocks held by device (r, c): block ids first, in slot order, then -1. Block b belongs to column group b // 24, and every block of column group c is held by exactly one device of that column group. Each device holds 1 to 11 blocks, the devices of a column group hold 24 blocks together, and in every column group one device holds 11 blocks and one holds 1. `block_cells`: fields 0 and 4 (density, pressure) lie in 0.7 to 1.4 and fields 1 to 3 (velocity) in -0.6 to 0.6. Slots marked -1 in slot_blocks hold values that no output depends on.
All inputs are finite; a program needn't handle non-finite values.
Results may differ from a plain program's by a relative error of at most 0.0001.
Values sent between devices are 32-bit elements; how exact they have to be, the bound alone decides.
A program may use at most 64 MiB of HBM per device.

v0:
```python
import jax
import jax.numpy as jnp
from jax import lax
from jax.sharding import PartitionSpec as P

BLK_MEAN = 6
OUT = 7
heat_ratio = 1.4
time_step = 0.12
thermal_leading_multiplier = 0.2
thermal_power_law_index = 0.7


def swapped(array, axis, apart):
    return lax.ppermute(array, axis, [(i, i ^ 1 << apart) for i in range(lax.axis_size(axis))])


def from_behind(block, axis, distance):
    devices = range(lax.axis_size(axis))
    route = [((i - distance) % len(devices), i) for i in devices]
    return lax.ppermute(block, axis, route)


def rebalance_table(anchors, counts):
    row_count, columns, slot_width = anchors.shape
    slot_ids = jnp.arange(slot_width, dtype=jnp.int32)
    row_ids = jnp.arange(row_count, dtype=jnp.int32)
    for section_bit in range(row_count.bit_length() - 1):
        partner = row_ids ^ 1 << section_bit
        other_anchors = anchors[partner]
        other_counts = counts[partner]
        sending = jnp.maximum(counts - other_counts, 0) // 2
        taking = jnp.maximum(other_counts - counts, 0) // 2
        keeping = (counts - sending)[:, :, None]
        anchor_slot = other_counts[:, :, None] - taking[:, :, None] + slot_ids - keeping
        pulled = jnp.take_along_axis(
            other_anchors, jnp.clip(anchor_slot, 0, slot_width - 1), axis=2
        )
        anchors = jnp.where(
            slot_ids < keeping,
            anchors,
            jnp.where(slot_ids < keeping + taking[:, :, None], pulled, -1),
        )
        counts = counts - sending + taking
    return (anchors, counts)


def to_conserved(primitive):
    matter_per_volume = primitive[0]
    velocity = primitive[1:4]
    fluid_static_stress = primitive[4]
    energy = fluid_static_stress / (heat_ratio - 1.0) + 0.5 * matter_per_volume * jnp.sum(
        velocity * velocity, axis=0
    )
    return jnp.concatenate(
        [matter_per_volume[None], matter_per_volume[None] * velocity, energy[None]], axis=0
    )


def to_primitive(conserved):
    matter_per_volume = conserved[0]
    velocity = conserved[1:4] / matter_per_volume
    fluid_static_stress = (heat_ratio - 1.0) * (
        conserved[4] - 0.5 * matter_per_volume * jnp.sum(velocity * velocity, axis=0)
    )
    return jnp.concatenate([matter_per_volume[None], velocity, fluid_static_stress[None]], axis=0)


def cell_terms(conserved, normal):
    matter_per_volume = conserved[0]
    momentum = conserved[1:4]
    velocity = momentum / matter_per_volume
    fluid_static_stress = (heat_ratio - 1.0) * (
        conserved[4] - 0.5 * matter_per_volume * jnp.sum(velocity * velocity, axis=0)
    )
    perpendicular_flow_rate = velocity[normal]
    moment_flux = momentum * perpendicular_flow_rate
    moment_flux = moment_flux.at[normal].add(fluid_static_stress)
    face_transport_amounts = jnp.concatenate(
        [
            momentum[normal][None],
            moment_flux,
            ((conserved[4] + fluid_static_stress) * perpendicular_flow_rate)[None],
        ],
        axis=0,
    )
    sound_signal_rate = jnp.sqrt(heat_ratio * fluid_static_stress / matter_per_volume)
    fluid_thermal_state = fluid_static_stress / matter_per_volume
    thermal_diffusivity_factor = thermal_leading_multiplier * jnp.power(
        fluid_thermal_state, thermal_power_law_index
    )
    return (
        face_transport_amounts,
        jnp.abs(perpendicular_flow_rate) + sound_signal_rate,
        fluid_thermal_state,
        thermal_diffusivity_factor,
        fluid_static_stress,
    )


def face_flux(lower_cons, lower_data, upper_cons, upper_data):
    wave_speed = jnp.maximum(lower_data[1], upper_data[1])
    face_transport_amounts = 0.5 * (lower_data[0] + upper_data[0]) - 0.5 * wave_speed[None] * (
        upper_cons - lower_cons
    )
    heat_flow = 0.5 * (lower_data[3] + upper_data[3]) * (upper_data[2] - lower_data[2])
    return face_transport_amounts.at[4].add(-heat_flow)


def wall_flux(fluid_static_stress, normal):
    nothing = jnp.zeros_like(fluid_static_stress)
    members = [nothing, nothing, nothing, nothing, nothing]
    members[normal + 1] = fluid_static_stress
    return jnp.stack(members, axis=0)


def cut_rows(tree, first_index, last_index):
    return jax.tree.map(lambda member: member[..., first_index:last_index, :], tree)


def cut_flat(tree, first_index, last_index):
    return jax.tree.map(lambda member: member[..., first_index:last_index], tree)


def block_tendency(conserved, low_x, high_x, low_y, high_y):
    block_edge = conserved.shape[1]
    flat_size = conserved.shape[2]
    padded_x = jnp.concatenate([low_x, conserved, high_x], axis=1)
    cell_data = cell_terms(padded_x, 0)
    face_transport_amounts = face_flux(
        padded_x[:, :-1],
        cut_rows(cell_data, 0, block_edge + 1),
        padded_x[:, 1:],
        cut_rows(cell_data, 1, block_edge + 2),
    )
    change_x = face_transport_amounts[:, 1:] - face_transport_amounts[:, :-1]
    padded_y = jnp.concatenate([low_y, conserved, high_y], axis=2)
    cell_data = cell_terms(padded_y, 1)
    reach_end = flat_size + block_edge
    face_transport_amounts = face_flux(
        padded_y[..., :reach_end],
        cut_flat(cell_data, 0, reach_end),
        padded_y[..., block_edge:],
        cut_flat(cell_data, block_edge, reach_end + block_edge),
    )
    change_y = face_transport_amounts[..., block_edge:] - face_transport_amounts[..., :flat_size]
    cell_data = cell_terms(conserved, 2)
    interior = face_flux(
        conserved[..., :-1],
        cut_flat(cell_data, 0, flat_size - 1),
        conserved[..., 1:],
        cut_flat(cell_data, 1, flat_size),
    )
    nothing = jnp.zeros_like(interior[..., :1])
    wall_values = wall_flux(cell_data[4], 2)
    height = jnp.arange(flat_size, dtype=jnp.int32) % block_edge
    upper_face = jnp.where(
        height == block_edge - 1, wall_values, jnp.concatenate([interior, nothing], axis=-1)
    )
    lower_face = jnp.where(height == 0, wall_values, jnp.concatenate([nothing, interior], axis=-1))
    change_z = upper_face - lower_face
    return -(change_x + change_y + change_z)


def body(block_cells, slot_blocks):
    row_count = lax.axis_size("row")
    columns = lax.axis_size("col")
    my_row = lax.axis_index("row")
    my_col = lax.axis_index("col")
    slot_width = slot_blocks.shape[1]
    per_group = BLK_MEAN * row_count
    send_slots = BLK_MEAN - 1
    block_edge = block_cells.shape[2]
    flat_size = block_cells.shape[3]
    every_slot = slot_blocks.reshape(-1)
    occupied = slot_blocks >= 0
    counts = jnp.sum(occupied.astype(jnp.int32), axis=1).reshape(row_count, columns)
    device_ids = jnp.arange(row_count * columns, dtype=jnp.int32)[:, None]
    anchors = jnp.where(
        occupied, device_ids * slot_width + jnp.arange(slot_width, dtype=jnp.int32)[None, :], -1
    )
    anchors = anchors.reshape(row_count, columns, slot_width)
    final_anchors, final_counts = rebalance_table(anchors, counts)
    final_anchors = final_anchors[:, :, :OUT]
    my_anchors = final_anchors[my_row, my_col]
    row_ids = jnp.arange(row_count, dtype=jnp.int32)
    holding = block_cells
    counts_now = counts
    slot_ids = jnp.arange(slot_width, dtype=jnp.int32)
    for section_bit in range(row_count.bit_length() - 1):
        partner = row_ids ^ 1 << section_bit
        other_counts = counts_now[partner]
        sending = jnp.maximum(counts_now - other_counts, 0) // 2
        taking = jnp.maximum(other_counts - counts_now, 0) // 2
        keeping = counts_now[my_row, my_col] - sending[my_row, my_col]
        send_from = jnp.clip(keeping + jnp.arange(send_slots, dtype=jnp.int32), 0, slot_width - 1)
        outgoing = jnp.take(holding, send_from, axis=0)
        incoming = swapped(outgoing, "row", section_bit)
        candidates = jnp.concatenate([holding, incoming], axis=0)
        chosen = jnp.where(
            slot_ids < keeping,
            slot_ids,
            slot_width + jnp.clip(slot_ids - keeping, 0, send_slots - 1),
        )
        holding = jnp.take(candidates, chosen, axis=0)
        counts_now = counts_now - sending + taking
    holding = holding[:OUT]
    active = my_anchors >= 0
    benign = jnp.array([1.0, 0.0, 0.0, 0.0, 1.0], jnp.float32)[None, :, None, None]
    holding = jnp.where(active[:, None, None, None], holding, benign)
    initial = jax.vmap(to_conserved)(holding)
    my_blocks = every_slot[jnp.maximum(my_anchors, 0)]
    along_y = jnp.clip(my_blocks - my_col * per_group, 0, per_group - 1)
    below_col = (my_col - 1) % columns
    above_col = (my_col + 1) % columns

    def located(column, wanted):
        anchors_here = final_anchors[:, column].reshape(-1)
        blocks_here = jnp.where(anchors_here >= 0, every_slot[jnp.maximum(anchors_here, 0)], -1)
        return jnp.argmax(blocks_here[None, :] == wanted[:, None], axis=1)

    from_x_low = located(below_col, below_col * per_group + along_y)
    from_y_low = located(below_col, below_col * per_group + (along_y - 1) % per_group)
    from_x_high = located(above_col, above_col * per_group + along_y)
    from_y_high = located(above_col, above_col * per_group + (along_y + 1) % per_group)

    def section_rate(current):
        highs = jnp.stack(
            [
                current[:, :, block_edge - 1, :],
                current[:, :, :, flat_size - block_edge :].reshape(OUT, 5, flat_size),
            ],
            axis=1,
        )
        lows = jnp.stack(
            [current[:, :, 0, :], current[:, :, :, :block_edge].reshape(OUT, 5, flat_size)], axis=1
        )
        passed_highs = from_behind(highs, "col", 1)
        passed_lows = from_behind(lows, "col", -1)
        from_below, from_above = (
            lax.all_gather(passed_highs, "row", axis=0, tiled=True),
            lax.all_gather(passed_lows, "row", axis=0, tiled=True),
        )
        low_x = from_below[from_x_low, 0][:, :, None, :]
        low_y = from_below[from_y_low, 1].reshape(OUT, 5, block_edge, block_edge)
        high_x = from_above[from_x_high, 0][:, :, None, :]
        high_y = from_above[from_y_high, 1].reshape(OUT, 5, block_edge, block_edge)
        return jax.vmap(block_tendency)(current, low_x, high_x, low_y, high_y)

    first_section = initial + time_step * section_rate(initial)
    second_section = 0.75 * initial + 0.25 * (
        first_section + time_step * section_rate(first_section)
    )
    third_section = 1.0 / 3.0 * initial + 2.0 / 3.0 * (
        second_section + time_step * section_rate(second_section)
    )
    result = jax.vmap(to_primitive)(third_section)
    return jnp.where(active[:, None, None, None], result, jnp.zeros_like(result)).astype(
        jnp.float32
    )


def solution(mesh):
    in_specs = (P(("row", "col"), None, None, None), P())
    out_specs = P(("row", "col"), None, None, None)
    return jax.shard_map(body, mesh=mesh, in_specs=in_specs, out_specs=out_specs, check_vma=False)
```

profile of v0, /device:TPU:0, one launch (start us, length us, event | category | flops | bytes accessed | tf_op | source)
XLA Modules:
  0.0 179.7 jit_solution(13251556273873494992)
XLA Ops:
  0.0 0.8 copy.142
  1.1 0.6 gather_fusion
  1.7 0.6 dynamic_slice.24
  2.3 0.7 dynamic_slice.26
  2.9 0.6 dynamic_slice.25
  4.7 0.6 gather_fusion.1
  5.3 0.6 dynamic_slice.27
  7.2 1.7 gather_fusion.21
  9.0 3.1 %collective-permute-start = (f32[5,5,16,256]{3,2,1,0:T(8,128)S(1)}, f32[5,5,16,256]{3,2,1,0:T(8,128)S(1)}, u32[]{:S(2)}, u32[]{:S(2)}) collective-permute-start(f32[5,5,16,256]{3,2,1,0:T(8,128)S(1)} %broadcast_select_fusion.2), channel_id=1, source_target_pairs={{0,8},{8,0},{16,24},{24,16},{1,9},{9,1},{17,25},{25,17},{2,10},{10... | collective-permute-start | bytes 1228808 | tf_op jit(solution)/shard_map/ppermute | solution.py:15
  12.5 0.6 gather_fusion.2
  13.4 4.0 %gather_fusion.19 = s32[352]{0:T(512)S(1)} fusion(s32[4,8,11]{2,1,0:T(8,128)S(1)} %gather_fusion.2, s32[352]{0:T(512)S(1)} %reshape.1164), kind=kCustom, calls=%fused_computation.clone | custom fusion | bytes 7040 | tf_op jit(solution)/shard_map/jit(take_along_axis)/gather | solution.py:36
  17.6 0.6 gather_fusion.3
  18.2 4.0 %gather_fusion.20 = s32[352]{0:T(512)S(1)} fusion(s32[4,8,11]{2,1,0:T(8,128)S(1)} %gather_fusion.3, s32[352]{0:T(512)S(1)} %reshape.1169), kind=kCustom, calls=%fused_computation.3.clone | custom fusion | bytes 7040 | tf_op jit(solution)/shard_map/jit(take_along_axis)/gather | solution.py:36
  22.9 0.7 gather_fusion.7
  23.6 0.7 gather_fusion.4
  24.3 0.6 gather_fusion.5
  25.0 0.7 iota_reduce_fusion.2
  25.7 0.7 iota_reduce_fusion
  26.5 0.7 iota_reduce_fusion.3
  27.2 0.7 iota_reduce_fusion.1
  28.0 0.6 gather_fusion.22
  28.8 0.6 gather_fusion.23
  29.5 2.7 %collective-permute-start.1 = (f32[5,5,16,256]{3,2,1,0:T(8,128)S(1)}, f32[5,5,16,256]{3,2,1,0:T(8,128)S(1)}, u32[]{:S(2)}, u32[]{:S(2)}) collective-permute-start(f32[5,5,16,256]{3,2,1,0:T(8,128)S(1)} %broadcast_select_fusion.1), channel_id=1, source_target_pairs={{0,16},{8,24},{16,0},{24,8},{1,17},{9,25},{17,1},{25,9},{2,18},{10... | collective-permute-start | bytes 1228808 | tf_op jit(solution)/shard_map/ppermute | solution.py:15
  32.1 17.8 %collective-permute-done.1 = f32[5,5,16,256]{3,2,1,0:T(8,128)S(1)} collective-permute-done((f32[5,5,16,256]{3,2,1,0:T(8,128)S(1)}, f32[5,5,16,256]{3,2,1,0:T(8,128)S(1)}, u32[]{:S(2)}, u32[]{:S(2)}) %collective-permute-start.1) | collective-permute-done | bytes 409632 | tf_op jit(solution)/shard_map/ppermute | solution.py:15
  50.1 0.6 gather_fusion.24
  52.2 2.2 %collective-permute-start.3 = (f32[7,2,5,256]{3,1,2,0:T(2,128)S(1)}, f32[7,2,5,256]{3,1,2,0:T(2,128)S(1)}, u32[]{:S(2)}, u32[]{:S(2)}) collective-permute-start(f32[7,2,5,256]{3,1,2,0:T(2,128)S(1)} %pad_maximum_fusion.29), channel_id=1, source_target_pairs={{1,0},{2,1},{3,2},{4,3},{5,4},{6,5},{7,6},{0,7},{9,8},{10,9},{11,1... | collective-permute-start | bytes 215048 | tf_op jit(solution)/shard_map/ppermute | solution.py:21
  54.6 0.4 fusion.59
  55.1 4.1 %collective-permute-done.2 = f32[7,2,5,256]{3,1,2,0:T(2,128)S(1)} collective-permute-done((f32[7,2,5,256]{3,1,2,0:T(2,128)S(1)}, f32[7,2,5,256]{3,1,2,0:T(2,128)S(1)}, u32[]{:S(2)}, u32[]{:S(2)}) %collective-permute-start.2) | collective-permute-done | bytes 71712 | tf_op jit(solution)/shard_map/ppermute | solution.py:21
  59.2 14.6 %all_gather.18 = f32[28,2,5,256]{3,1,2,0:T(2,128)S(1)} all-gather(f32[7,2,5,256]{3,1,2,0:T(2,128)S(1)} %collective-permute-done.2), channel_id=1, replica_groups=mesh['row'=4,'col'=8] {'row'}, dimensions={0}, use_global_device_ids=true | all-gather | bytes 358400 | tf_op jit(solution)/shard_map/all_gather | solution.py:241
  73.8 0.6 gather_fusion.9
  74.4 13.9 %all_gather.19 = f32[28,2,5,256]{3,1,2,0:T(2,128)S(1)} all-gather(f32[7,2,5,256]{3,1,2,0:T(2,128)S(1)} %collective-permute-done.3), channel_id=1, replica_groups=mesh['row'=4,'col'=8] {'row'}, dimensions={0}, use_global_device_ids=true | all-gather | bytes 358400 | tf_op jit(solution)/shard_map/all_gather | solution.py:242
  88.4 0.6 gather_fusion.10
  89.4 0.4 pad_maximum_fusion.6
  89.8 0.6 gather_fusion.6
  90.4 1.6 gather_fusion.8
  93.6 0.5 fusion.17
  94.3 0.3 fusion.25
  94.9 0.5 fusion.65
  96.8 0.7 collective-permute-start.4
  97.5 0.4 fusion.49
  98.1 3.6 %collective-permute-done.4 = f32[7,2,5,256]{3,1,2,0:T(2,128)S(1)} collective-permute-done((f32[7,2,5,256]{3,1,2,0:T(2,128)S(1)}, f32[7,2,5,256]{3,1,2,0:T(2,128)S(1)}, u32[]{:S(2)}, u32[]{:S(2)}) %collective-permute-start.4) | collective-permute-done | bytes 71712 | tf_op jit(solution)/shard_map/ppermute | solution.py:21
  101.7 14.2 %all_gather.20 = f32[28,2,5,256]{3,1,2,0:T(2,128)S(1)} all-gather(f32[7,2,5,256]{3,1,2,0:T(2,128)S(1)} %collective-permute-done.4), channel_id=1, replica_groups=mesh['row'=4,'col'=8] {'row'}, dimensions={0}, use_global_device_ids=true | all-gather | bytes 358400 | tf_op jit(solution)/shard_map/all_gather | solution.py:241
  115.9 0.6 gather_fusion.13
  116.5 0.6 gather_fusion.11
  117.1 14.4 %all_gather.21 = f32[28,2,5,256]{3,1,2,0:T(2,128)S(1)} all-gather(f32[7,2,5,256]{3,1,2,0:T(2,128)S(1)} %collective-permute-done.5), channel_id=1, replica_groups=mesh['row'=4,'col'=8] {'row'}, dimensions={0}, use_global_device_ids=true | all-gather | bytes 358400 | tf_op jit(solution)/shard_map/all_gather | solution.py:242
  131.6 0.6 gather_fusion.14
  132.2 0.6 gather_fusion.12
  133.2 0.4 pad_maximum_fusion.8
  135.3 0.5 fusion.9
  135.9 0.3 fusion.13
  136.5 0.6 fusion.57
  138.5 0.5 collective-permute-start.6
  139.1 0.4 fusion.39
  139.6 3.6 %collective-permute-done.6 = f32[7,2,5,256]{3,1,2,0:T(2,128)S(1)} collective-permute-done((f32[7,2,5,256]{3,1,2,0:T(2,128)S(1)}, f32[7,2,5,256]{3,1,2,0:T(2,128)S(1)}, u32[]{:S(2)}, u32[]{:S(2)}) %collective-permute-start.6) | collective-permute-done | bytes 71712 | tf_op jit(solution)/shard_map/ppermute | solution.py:21
  143.2 14.1 %all_gather.22 = f32[28,2,5,256]{3,1,2,0:T(2,128)S(1)} all-gather(f32[7,2,5,256]{3,1,2,0:T(2,128)S(1)} %collective-permute-done.6), channel_id=1, replica_groups=mesh['row'=4,'col'=8] {'row'}, dimensions={0}, use_global_device_ids=true | all-gather | bytes 358400 | tf_op jit(solution)/shard_map/all_gather | solution.py:241
  157.4 0.6 gather_fusion.17
  158.0 0.6 gather_fusion.15
  158.6 14.4 %all_gather.23 = f32[28,2,5,256]{3,1,2,0:T(2,128)S(1)} all-gather(f32[7,2,5,256]{3,1,2,0:T(2,128)S(1)} %collective-permute-done.7), channel_id=1, replica_groups=mesh['row'=4,'col'=8] {'row'}, dimensions={0}, use_global_device_ids=true | all-gather | bytes 358400 | tf_op jit(solution)/shard_map/all_gather | solution.py:242
  173.1 0.6 gather_fusion.18
  173.7 0.6 gather_fusion.16
  174.7 0.4 pad_maximum_fusion.10
  176.7 0.5 fusion.1
  178.0 0.6 fusion.47
  178.9 0.8 copy.184
  (225 shorter events, 15.1 us)
Async XLA Ops:
  9.0 18.9 %collective-permute-start = (f32[5,5,16,256]{3,2,1,0:T(8,128)S(1)}, f32[5,5,16,256]{3,2,1,0:T(8,128)S(1)}, u32[]{:S(2)}, u32[]{:S(2)}) collective-permute-start(f32[5,5,16,256]{3,2,1,0:T(8,128)S(1)} %broadcast_select_fusion.2), channel_id=1, source_target_pairs={{0,8},{8,0},{16,24},{24,16},{1,9},{9,1},{17,25},{25,17},{2,10},{10... | collective-permute-start | bytes 1228808 | tf_op jit(solution)/shard_map/ppermute | solution.py:15
  22.2 5.7 %copy-start = (f32[11,5,16,256]{3,2,1,0:T(8,128)S(1)}, f32[11,5,16,256]{3,2,1,0:T(8,128)}, u32[]{:S(2)}) copy-start(f32[11,5,16,256]{3,2,1,0:T(8,128)} %param.45) | copy-start | bytes 2703364
  29.5 20.5 %collective-permute-start.1 = (f32[5,5,16,256]{3,2,1,0:T(8,128)S(1)}, f32[5,5,16,256]{3,2,1,0:T(8,128)S(1)}, u32[]{:S(2)}, u32[]{:S(2)}) collective-permute-start(f32[5,5,16,256]{3,2,1,0:T(8,128)S(1)} %broadcast_select_fusion.1), channel_id=1, source_target_pairs={{0,16},{8,24},{16,0},{24,8},{1,17},{9,25},{17,1},{25,9},{2,18},{10... | collective-permute-start | bytes 1228808 | tf_op jit(solution)/shard_map/ppermute | solution.py:15
  50.1 0.7 copy-start.2
  52.2 22.2 %collective-permute-start.3 = (f32[7,2,5,256]{3,1,2,0:T(2,128)S(1)}, f32[7,2,5,256]{3,1,2,0:T(2,128)S(1)}, u32[]{:S(2)}, u32[]{:S(2)}) collective-permute-start(f32[7,2,5,256]{3,1,2,0:T(2,128)S(1)} %pad_maximum_fusion.29), channel_id=1, source_target_pairs={{1,0},{2,1},{3,2},{4,3},{5,4},{6,5},{7,6},{0,7},{9,8},{10,9},{11,1... | collective-permute-start | bytes 215048 | tf_op jit(solution)/shard_map/ppermute | solution.py:21
  54.5 4.7 %collective-permute-start.2 = (f32[7,2,5,256]{3,1,2,0:T(2,128)S(1)}, f32[7,2,5,256]{3,1,2,0:T(2,128)S(1)}, u32[]{:S(2)}, u32[]{:S(2)}) collective-permute-start(f32[7,2,5,256]{3,1,2,0:T(2,128)S(1)} %pad_maximum_fusion.28), channel_id=1, source_target_pairs={{7,0},{0,1},{1,2},{2,3},{3,4},{4,5},{5,6},{6,7},{15,8},{8,9},{9,10... | collective-permute-start | bytes 215048 | tf_op jit(solution)/shard_map/ppermute | solution.py:21
  88.4 0.8 copy-start.1
  96.6 20.5 %collective-permute-start.5 = (f32[7,2,5,256]{3,1,2,0:T(2,128)S(1)}, f32[7,2,5,256]{3,1,2,0:T(2,128)S(1)}, u32[]{:S(2)}, u32[]{:S(2)}) collective-permute-start(f32[7,2,5,256]{3,1,2,0:T(2,128)S(1)} %pad_maximum_fusion.31), channel_id=1, source_target_pairs={{1,0},{2,1},{3,2},{4,3},{5,4},{6,5},{7,6},{0,7},{9,8},{10,9},{11,1... | collective-permute-start | bytes 215048 | tf_op jit(solution)/shard_map/ppermute | solution.py:21
  96.8 4.9 %collective-permute-start.4 = (f32[7,2,5,256]{3,1,2,0:T(2,128)S(1)}, f32[7,2,5,256]{3,1,2,0:T(2,128)S(1)}, u32[]{:S(2)}, u32[]{:S(2)}) collective-permute-start(f32[7,2,5,256]{3,1,2,0:T(2,128)S(1)} %pad_maximum_fusion.30), channel_id=1, source_target_pairs={{7,0},{0,1},{1,2},{2,3},{3,4},{4,5},{5,6},{6,7},{15,8},{8,9},{9,10... | collective-permute-start | bytes 215048 | tf_op jit(solution)/shard_map/ppermute | solution.py:21
  138.3 20.2 %collective-permute-start.7 = (f32[7,2,5,256]{3,1,2,0:T(2,128)S(1)}, f32[7,2,5,256]{3,1,2,0:T(2,128)S(1)}, u32[]{:S(2)}, u32[]{:S(2)}) collective-permute-start(f32[7,2,5,256]{3,1,2,0:T(2,128)S(1)} %pad_maximum_fusion.33), channel_id=1, source_target_pairs={{1,0},{2,1},{3,2},{4,3},{5,4},{6,5},{7,6},{0,7},{9,8},{10,9},{11,1... | collective-permute-start | bytes 215048 | tf_op jit(solution)/shard_map/ppermute | solution.py:21
  138.5 4.7 %collective-permute-start.6 = (f32[7,2,5,256]{3,1,2,0:T(2,128)S(1)}, f32[7,2,5,256]{3,1,2,0:T(2,128)S(1)}, u32[]{:S(2)}, u32[]{:S(2)}) collective-permute-start(f32[7,2,5,256]{3,1,2,0:T(2,128)S(1)} %pad_maximum_fusion.32), channel_id=1, source_target_pairs={{7,0},{0,1},{1,2},{2,3},{3,4},{4,5},{5,6},{6,7},{15,8},{8,9},{9,10... | collective-permute-start | bytes 215048 | tf_op jit(solution)/shard_map/ppermute | solution.py:21
where the time goes:
time: 180 us
  blocking collectives  85.5 us (48%)
  local copies, waits for them, and re-layouts  32.5 us (18%)
  waiting for transfers between devices  29.1 us (16%)
  other arithmetic  19.2 us (11%)
  starting transfers between devices  9.39 us (5%)
  between operations  3.94 us (2%)
    all_gather x3, blocking collectives, section_rate(): lax.all_gather(passed_highs, 'row', axis=0, tiled=True)  42.9 us
    all_gather x3, blocking collectives, section_rate(): lax.all_gather(passed_lows, 'row', axis=0, tiled=True)  42.7 us
    ppermute x2, waiting for transfers between devices, swapped(): lax.ppermute(array, axis, [(i, i ^ 1 << apart) for i in range(lax.axis_si...  17.8 us
    ppermute x6, waiting for transfers between devices, from_behind(): return lax.ppermute(block, axis, route)  11.3 us
    gather x6, local copies, waits for them, and re-layouts, rebalance_table(): jnp.take_along_axis(other_anchors, jnp.clip(anchor_slot, 0, slot_width -...  8.44 us
    ppermute x2, starting transfers between devices, swapped(): lax.ppermute(array, axis, [(i, i ^ 1 << apart) for i in range(lax.axis_si...  5.78 us
    sub x9, other arithmetic, face_flux(): 0.5 * (lower_data[0] + upper_data[0])  3.63 us
    ppermute x6, starting transfers between devices, from_behind(): return lax.ppermute(block, axis, route)  3.61 us
  transfers between devices with their start and end apart: 8, of which 4 were waited for; matrix products, arithmetic and copies ran while one was open for 11% of the time, Pallas kernels for 0%

commit v1 on v0

--- a/solution.py
+++ b/solution.py
@@ -9,6 +9,17 @@
 time_step = 0.12
 thermal_leading_multiplier = 0.2
 thermal_power_law_index = 0.7
+
+
+def ring_gather(value, axis, dim):
+    ways = lax.axis_size(axis)
+    pieces = [value]
+    for far in range(1, ways):
+        pieces.append(
+            lax.ppermute(pieces[far - 1], axis, [(d, (d - 1) % ways) for d in range(ways)])
+        )
+    line = jnp.concatenate(pieces, axis=dim)
+    return jnp.roll(line, lax.axis_index(axis) * value.shape[dim], axis=dim)
 
 
 def swapped(array, axis, apart):
@@ -238,7 +249,7 @@
         passed_highs = from_behind(highs, "col", 1)
         passed_lows = from_behind(lows, "col", -1)
         from_below, from_above = (
-            lax.all_gather(passed_highs, "row", axis=0, tiled=True),
+            ring_gather(passed_highs, "row", 0),
             lax.all_gather(passed_lows, "row", axis=0, tiled=True),
         )
         low_x = from_below[from_x_low, 0][:, :, None, :]

time: 180 us -> 189 us (1.050)
  blocking collectives: 85.5 us -> 43.8 us
  waiting for transfers between devices: 29.1 us -> 53.1 us
  starting transfers between devices: 9.39 us -> 30.8 us
  other arithmetic: 19.2 us -> 23 us
    all_gather x3 -> x0, blocking collectives: 42.9 us -> none  [section_rate(): lax.all_gather(passed_highs, 'row', axis=0, tiled=True)]
    ppermute x0 -> x9, starting transfers between devices: none -> 21.6 us  [ring_gather(): lax.ppermute(pieces[far - 1], axis, [(d, (d - 1) % ways) for d in range(w...]
    ppermute x0 -> x9, waiting for transfers between devices: none -> 21 us  [ring_gather(): lax.ppermute(pieces[far - 1], axis, [(d, (d - 1) % ways) for d in range(w...]
    concatenate x0 -> x5, other arithmetic: none -> 4.02 us  [the longest x3 4.01 us: ring_gather(): return jnp.roll(line, lax.axis_index(axis) * value.shape[dim], axis=dim)]
    ppermute x6, waiting for transfers between devices: 11.3 us -> 14.2 us  [from_behind(): return lax.ppermute(block, axis, route)]
  transfers between devices with their start and end apart: 8 -> 17, of which waited for: 4 -> 10; matrix products, arithmetic and copies ran while one was open for 11% -> 11% of each run, Pallas kernels for 0% -> 0%
where the time goes in v1:
time: 189 us; the launch traced here: 188 us
  waiting for transfers between devices  53.1 us (28%)
  blocking collectives  43.8 us (23%)
  local copies, waits for them, and re-layouts  33.6 us (18%)
  starting transfers between devices  30.8 us (16%)
  other arithmetic  23 us (12%)
  between operations  4.12 us (2%)
    all_gather x3, blocking collectives, section_rate(): lax.all_gather(passed_lows, 'row', axis=0, tiled=True)  43.8 us
    ppermute x9, starting transfers between devices, ring_gather(): lax.ppermute(pieces[far - 1], axis, [(d, (d - 1) % ways) for d in range(w...  21.6 us
    ppermute x9, waiting for transfers between devices, ring_gather(): lax.ppermute(pieces[far - 1], axis, [(d, (d - 1) % ways) for d in range(w...  21 us
    ppermute x2, waiting for transfers between devices, swapped(): lax.ppermute(array, axis, [(i, i ^ 1 << apart) for i in range(lax.axis_si...  17.8 us
    ppermute x6, waiting for transfers between devices, from_behind(): return lax.ppermute(block, axis, route)  14.2 us
    gather x6, local copies, waits for them, and re-layouts, rebalance_table(): jnp.take_along_axis(other_anchors, jnp.clip(anchor_slot, 0, slot_width -...  8.44 us
    ppermute x2, starting transfers between devices, swapped(): lax.ppermute(array, axis, [(i, i ^ 1 << apart) for i in range(lax.axis_si...  5.78 us
    concatenate x3, other arithmetic, ring_gather(): return jnp.roll(line, lax.axis_index(axis) * value.shape[dim], axis=dim)  4.01 us
  transfers between devices with their start and end apart: 17, of which 10 were waited for; matrix products, arithmetic and copies ran while one was open for 11% of the time, Pallas kernels for 0%

profile of v1, /device:TPU:0, one launch (start us, length us, event | category | flops | bytes accessed | tf_op | source)
XLA Modules:
  0.0 188.4 jit_solution(10025840510987472508)
XLA Ops:
  0.0 0.8 copy.139
  1.1 0.6 gather_fusion
  1.7 0.6 dynamic_slice.27
  2.3 0.7 dynamic_slice.29
  2.9 0.6 dynamic_slice.28
  4.7 0.6 gather_fusion.1
  5.3 0.6 dynamic_slice.30
  7.2 1.7 gather_fusion.21
  9.0 3.1 %collective-permute-start = (f32[5,5,16,256]{3,2,1,0:T(8,128)S(1)}, f32[5,5,16,256]{3,2,1,0:T(8,128)S(1)}, u32[]{:S(2)}, u32[]{:S(2)}) collective-permute-start(f32[5,5,16,256]{3,2,1,0:T(8,128)S(1)} %broadcast_select_fusion.2), channel_id=1, source_target_pairs={{0,8},{8,0},{16,24},{24,16},{1,9},{9,1},{17,25},{25,17},{2,10},{10... | collective-permute-start | bytes 1228808 | tf_op jit(solution)/shard_map/ppermute | solution.py:26
  12.4 0.6 gather_fusion.2
  13.3 4.0 %gather_fusion.19 = s32[352]{0:T(512)S(1)} fusion(s32[4,8,11]{2,1,0:T(8,128)S(1)} %gather_fusion.2, s32[352]{0:T(512)S(1)} %reshape.1164), kind=kCustom, calls=%fused_computation.clone | custom fusion | bytes 7040 | tf_op jit(solution)/shard_map/jit(take_along_axis)/gather | solution.py:47
  18.1 4.0 %gather_fusion.20 = s32[352]{0:T(512)S(1)} fusion(s32[4,8,11]{2,1,0:T(8,128)S(1)} %gather_fusion.3, s32[352]{0:T(512)S(1)} %reshape.1169), kind=kCustom, calls=%fused_computation.3.clone | custom fusion | bytes 7040 | tf_op jit(solution)/shard_map/jit(take_along_axis)/gather | solution.py:47
  22.9 0.7 gather_fusion.7
  23.6 0.7 gather_fusion.4
  24.3 0.6 gather_fusion.5
  25.0 0.7 iota_reduce_fusion.2
  25.7 0.7 iota_reduce_fusion
  26.5 0.7 iota_reduce_fusion.3
  27.2 0.7 iota_reduce_fusion.1
  28.0 0.6 gather_fusion.22
  28.7 0.6 gather_fusion.23
  29.4 2.7 %collective-permute-start.1 = (f32[5,5,16,256]{3,2,1,0:T(8,128)S(1)}, f32[5,5,16,256]{3,2,1,0:T(8,128)S(1)}, u32[]{:S(2)}, u32[]{:S(2)}) collective-permute-start(f32[5,5,16,256]{3,2,1,0:T(8,128)S(1)} %broadcast_select_fusion.1), channel_id=1, source_target_pairs={{0,16},{8,24},{16,0},{24,8},{1,17},{9,25},{17,1},{25,9},{2,18},{10... | collective-permute-start | bytes 1228808 | tf_op jit(solution)/shard_map/ppermute | solution.py:26
  32.1 17.8 %collective-permute-done.1 = f32[5,5,16,256]{3,2,1,0:T(8,128)S(1)} collective-permute-done((f32[5,5,16,256]{3,2,1,0:T(8,128)S(1)}, f32[5,5,16,256]{3,2,1,0:T(8,128)S(1)}, u32[]{:S(2)}, u32[]{:S(2)}) %collective-permute-start.1) | collective-permute-done | bytes 409632 | tf_op jit(solution)/shard_map/ppermute | solution.py:26
  50.0 0.6 gather_fusion.24
  52.2 2.2 %collective-permute-start.6 = (f32[7,2,5,256]{3,1,2,0:T(2,128)S(1)}, f32[7,2,5,256]{3,1,2,0:T(2,128)S(1)}, u32[]{:S(2)}, u32[]{:S(2)}) collective-permute-start(f32[7,2,5,256]{3,1,2,0:T(2,128)S(1)} %pad_maximum_fusion.31), channel_id=1, source_target_pairs={{1,0},{2,1},{3,2},{4,3},{5,4},{6,5},{7,6},{0,7},{9,8},{10,9},{11,1... | collective-permute-start | bytes 215048 | tf_op jit(solution)/shard_map/ppermute | solution.py:32
  54.5 5.1 %collective-permute-done.2 = f32[7,2,5,256]{3,2,1,0:T(8,128)S(1)} collective-permute-done((f32[7,2,5,256]{3,2,1,0:T(8,128)S(1)}, f32[7,2,5,256]{3,2,1,0:T(8,128)S(1)}, u32[]{:S(2)}, u32[]{:S(2)}) %collective-permute-start.2) | collective-permute-done | bytes 71712 | tf_op jit(solution)/shard_map/ppermute | solution.py:32
  59.5 1.6 collective-permute-start.3
  61.5 4.0 %collective-permute-done.3 = f32[7,2,5,256]{3,2,1,0:T(8,128)S(1)} collective-permute-done((f32[7,2,5,256]{3,2,1,0:T(8,128)S(1)}, f32[7,2,5,256]{3,2,1,0:T(8,128)S(1)}, u32[]{:S(2)}, u32[]{:S(2)}) %collective-permute-start.3) | collective-permute-done | bytes 71712 | tf_op jit(solution)/shard_map/ppermute | solution.py:19
  65.5 2.2 %collective-permute-start.4 = (f32[7,2,5,256]{3,2,1,0:T(8,128)S(1)}, f32[7,2,5,256]{3,2,1,0:T(8,128)S(1)}, u32[]{:S(2)}, u32[]{:S(2)}) collective-permute-start(f32[7,2,5,256]{3,2,1,0:T(8,128)S(1)} %collective-permute-done.3), channel_id=1, source_target_pairs={{0,24},{8,0},{16,8},{24,16},{1,25},{9,1},{17,9},{25,17},{2,26},{10... | collective-permute-start | bytes 215048 | tf_op jit(solution)/shard_map/ppermute | solution.py:19
  67.8 3.2 %collective-permute-done.4 = f32[7,2,5,256]{3,2,1,0:T(8,128)S(1)} collective-permute-done((f32[7,2,5,256]{3,2,1,0:T(8,128)S(1)}, f32[7,2,5,256]{3,2,1,0:T(8,128)S(1)}, u32[]{:S(2)}, u32[]{:S(2)}) %collective-permute-start.4) | collective-permute-done | bytes 71712 | tf_op jit(solution)/shard_map/ppermute | solution.py:19
  71.1 3.3 %collective-permute-start.5 = (f32[7,2,5,256]{3,2,1,0:T(8,128)S(1)}, f32[7,2,5,256]{3,2,1,0:T(8,128)S(1)}, u32[]{:S(2)}, u32[]{:S(2)}) collective-permute-start(f32[7,2,5,256]{3,2,1,0:T(8,128)S(1)} %collective-permute-done.4), channel_id=1, source_target_pairs={{0,24},{8,0},{16,8},{24,16},{1,25},{9,1},{17,9},{25,17},{2,26},{10... | collective-permute-start | bytes 215048 | tf_op jit(solution)/shard_map/ppermute | solution.py:19
  74.4 14.5 %all_gather.9 = f32[28,2,5,256]{3,1,2,0:T(2,128)S(1)} all-gather(f32[7,2,5,256]{3,1,2,0:T(2,128)S(1)} %collective-permute-done.6), channel_id=1, replica_groups=mesh['row'=4,'col'=8] {'row'}, dimensions={0}, use_global_device_ids=true | all-gather | bytes 358400 | tf_op jit(solution)/shard_map/all_gather | solution.py:253
  89.0 0.6 gather_fusion.10
  89.6 0.6 gather_fusion.8
  90.4 1.6 fusion.95
  92.0 1.6 gather_fusion.9
  94.3 1.6 gather_fusion.6
  101.2 4.6 %collective-permute-done.7 = f32[7,2,5,256]{3,2,1,0:T(8,128)S(1)} collective-permute-done((f32[7,2,5,256]{3,2,1,0:T(8,128)S(1)}, f32[7,2,5,256]{3,2,1,0:T(8,128)S(1)}, u32[]{:S(2)}, u32[]{:S(2)}) %collective-permute-start.7) | collective-permute-done | bytes 71712 | tf_op jit(solution)/shard_map/ppermute | solution.py:32
  105.8 1.4 collective-permute-start.8
  107.6 3.7 %collective-permute-done.8 = f32[7,2,5,256]{3,2,1,0:T(8,128)S(1)} collective-permute-done((f32[7,2,5,256]{3,2,1,0:T(8,128)S(1)}, f32[7,2,5,256]{3,2,1,0:T(8,128)S(1)}, u32[]{:S(2)}, u32[]{:S(2)}) %collective-permute-start.8) | collective-permute-done | bytes 71712 | tf_op jit(solution)/shard_map/ppermute | solution.py:19
  111.3 2.5 %collective-permute-start.9 = (f32[7,2,5,256]{3,2,1,0:T(8,128)S(1)}, f32[7,2,5,256]{3,2,1,0:T(8,128)S(1)}, u32[]{:S(2)}, u32[]{:S(2)}) collective-permute-start(f32[7,2,5,256]{3,2,1,0:T(8,128)S(1)} %collective-permute-done.8), channel_id=1, source_target_pairs={{0,24},{8,0},{16,8},{24,16},{1,25},{9,1},{17,9},{25,17},{2,26},{10... | collective-permute-start | bytes 215048 | tf_op jit(solution)/shard_map/ppermute | solution.py:19
  113.9 3.2 %collective-permute-done.9 = f32[7,2,5,256]{3,2,1,0:T(8,128)S(1)} collective-permute-done((f32[7,2,5,256]{3,2,1,0:T(8,128)S(1)}, f32[7,2,5,256]{3,2,1,0:T(8,128)S(1)}, u32[]{:S(2)}, u32[]{:S(2)}) %collective-permute-start.9) | collective-permute-done | bytes 71712 | tf_op jit(solution)/shard_map/ppermute | solution.py:19
  117.1 3.3 %collective-permute-start.10 = (f32[7,2,5,256]{3,2,1,0:T(8,128)S(1)}, f32[7,2,5,256]{3,2,1,0:T(8,128)S(1)}, u32[]{:S(2)}, u32[]{:S(2)}) collective-permute-start(f32[7,2,5,256]{3,2,1,0:T(8,128)S(1)} %collective-permute-done.9), channel_id=1, source_target_pairs={{0,24},{8,0},{16,8},{24,16},{1,25},{9,1},{17,9},{25,17},{2,26},{10... | collective-permute-start | bytes 215048 | tf_op jit(solution)/shard_map/ppermute | solution.py:19
  120.5 14.6 %all_gather.10 = f32[28,2,5,256]{3,1,2,0:T(2,128)S(1)} all-gather(f32[7,2,5,256]{3,1,2,0:T(2,128)S(1)} %collective-permute-done.11), channel_id=1, replica_groups=mesh['row'=4,'col'=8] {'row'}, dimensions={0}, use_global_device_ids=true | all-gather | bytes 358400 | tf_op jit(solution)/shard_map/all_gather | solution.py:253
  135.1 0.6 gather_fusion.14
  135.7 0.6 gather_fusion.12
  136.5 1.6 fusion.88
  138.2 0.6 gather_fusion.11
  138.8 0.6 gather_fusion.13
  143.0 0.6 fusion.57
  145.4 4.6 %collective-permute-done.12 = f32[7,2,5,256]{3,2,1,0:T(8,128)S(1)} collective-permute-done((f32[7,2,5,256]{3,2,1,0:T(8,128)S(1)}, f32[7,2,5,256]{3,2,1,0:T(8,128)S(1)}, u32[]{:S(2)}, u32[]{:S(2)}) %collective-permute-start.12) | collective-permute-done | bytes 71712 | tf_op jit(solution)/shard_map/ppermute | solution.py:32
  150.0 1.4 collective-permute-start.13
  151.7 3.7 %collective-permute-done.13 = f32[7,2,5,256]{3,2,1,0:T(8,128)S(1)} collective-permute-done((f32[7,2,5,256]{3,2,1,0:T(8,128)S(1)}, f32[7,2,5,256]{3,2,1,0:T(8,128)S(1)}, u32[]{:S(2)}, u32[]{:S(2)}) %collective-permute-start.13) | collective-permute-done | bytes 71712 | tf_op jit(solution)/shard_map/ppermute | solution.py:19
  155.5 2.5 %collective-permute-start.14 = (f32[7,2,5,256]{3,2,1,0:T(8,128)S(1)}, f32[7,2,5,256]{3,2,1,0:T(8,128)S(1)}, u32[]{:S(2)}, u32[]{:S(2)}) collective-permute-start(f32[7,2,5,256]{3,2,1,0:T(8,128)S(1)} %collective-permute-done.13), channel_id=1, source_target_pairs={{0,24},{8,0},{16,8},{24,16},{1,25},{9,1},{17,9},{25,17},{2,26},{10... | collective-permute-start | bytes 215048 | tf_op jit(solution)/shard_map/ppermute | solution.py:19
  158.1 3.2 %collective-permute-done.14 = f32[7,2,5,256]{3,2,1,0:T(8,128)S(1)} collective-permute-done((f32[7,2,5,256]{3,2,1,0:T(8,128)S(1)}, f32[7,2,5,256]{3,2,1,0:T(8,128)S(1)}, u32[]{:S(2)}, u32[]{:S(2)}) %collective-permute-start.14) | collective-permute-done | bytes 71712 | tf_op jit(solution)/shard_map/ppermute | solution.py:19
  161.3 3.4 %collective-permute-start.15 = (f32[7,2,5,256]{3,2,1,0:T(8,128)S(1)}, f32[7,2,5,256]{3,2,1,0:T(8,128)S(1)}, u32[]{:S(2)}, u32[]{:S(2)}) collective-permute-start(f32[7,2,5,256]{3,2,1,0:T(8,128)S(1)} %collective-permute-done.14), channel_id=1, source_target_pairs={{0,24},{8,0},{16,8},{24,16},{1,25},{9,1},{17,9},{25,17},{2,26},{10... | collective-permute-start | bytes 215048 | tf_op jit(solution)/shard_map/ppermute | solution.py:19
  164.7 14.7 %all_gather.11 = f32[28,2,5,256]{3,1,2,0:T(2,128)S(1)} all-gather(f32[7,2,5,256]{3,1,2,0:T(2,128)S(1)} %collective-permute-done.16), channel_id=1, replica_groups=mesh['row'=4,'col'=8] {'row'}, dimensions={0}, use_global_device_ids=true | all-gather | bytes 358400 | tf_op jit(solution)/shard_map/all_gather | solution.py:253
  179.4 0.6 gather_fusion.18
  180.0 0.6 gather_fusion.16
  180.9 0.8 fusion.81
  181.7 0.6 gather_fusion.15
  182.3 0.6 gather_fusion.17
  186.8 0.6 fusion.47
  187.6 0.8 copy.178
  (278 shorter events, 21.6 us)
Async XLA Ops:
  9.0 18.8 %collective-permute-start = (f32[5,5,16,256]{3,2,1,0:T(8,128)S(1)}, f32[5,5,16,256]{3,2,1,0:T(8,128)S(1)}, u32[]{:S(2)}, u32[]{:S(2)}) collective-permute-start(f32[5,5,16,256]{3,2,1,0:T(8,128)S(1)} %broadcast_select_fusion.2), channel_id=1, source_target_pairs={{0,8},{8,0},{16,24},{24,16},{1,9},{9,1},{17,25},{25,17},{2,10},{10... | collective-permute-start | bytes 1228808 | tf_op jit(solution)/shard_map/ppermute | solution.py:26
  12.2 130.8 %copy-start.13 = (pred[256]{0:T(512)(128)(4,1)}, pred[256]{0:T(512)(128)(4,1)S(1)}, u32[]{:S(2)}) copy-start(pred[256]{0:T(512)(128)(4,1)S(1)} %get-tuple-element.345) | copy-start | bytes 772
  12.2 130.8 %copy-start.15 = (pred[256]{0:T(512)(128)(4,1)}, pred[256]{0:T(512)(128)(4,1)S(1)}, u32[]{:S(2)}) copy-start(pred[256]{0:T(512)(128)(4,1)S(1)} %get-tuple-element.346) | copy-start | bytes 772
  22.1 5.8 %copy-start = (f32[11,5,16,256]{3,2,1,0:T(8,128)S(1)}, f32[11,5,16,256]{3,2,1,0:T(8,128)}, u32[]{:S(2)}) copy-start(f32[11,5,16,256]{3,2,1,0:T(8,128)} %param.47) | copy-start | bytes 2703364
  26.5 116.5 %copy-start.17 = (f32[5]{0:T(128)}, f32[5]{0:T(128)S(1)}, u32[]{:S(2)}) copy-start(f32[5]{0:T(128)S(1)} %pad.131.clone) | copy-start | bytes 64
  29.4 20.5 %collective-permute-start.1 = (f32[5,5,16,256]{3,2,1,0:T(8,128)S(1)}, f32[5,5,16,256]{3,2,1,0:T(8,128)S(1)}, u32[]{:S(2)}, u32[]{:S(2)}) collective-permute-start(f32[5,5,16,256]{3,2,1,0:T(8,128)S(1)} %broadcast_select_fusion.1), channel_id=1, source_target_pairs={{0,16},{8,24},{16,0},{24,8},{1,17},{9,25},{17,1},{25,9},{2,18},{10... | collective-permute-start | bytes 1228808 | tf_op jit(solution)/shard_map/ppermute | solution.py:26
  50.0 0.7 copy-start.19
  52.2 22.2 %collective-permute-start.6 = (f32[7,2,5,256]{3,1,2,0:T(2,128)S(1)}, f32[7,2,5,256]{3,1,2,0:T(2,128)S(1)}, u32[]{:S(2)}, u32[]{:S(2)}) collective-permute-start(f32[7,2,5,256]{3,1,2,0:T(2,128)S(1)} %pad_maximum_fusion.31), channel_id=1, source_target_pairs={{1,0},{2,1},{3,2},{4,3},{5,4},{6,5},{7,6},{0,7},{9,8},{10,9},{11,1... | collective-permute-start | bytes 215048 | tf_op jit(solution)/shard_map/ppermute | solution.py:32
  54.4 5.2 %collective-permute-start.2 = (f32[7,2,5,256]{3,2,1,0:T(8,128)S(1)}, f32[7,2,5,256]{3,2,1,0:T(8,128)S(1)}, u32[]{:S(2)}, u32[]{:S(2)}) collective-permute-start(f32[7,2,5,256]{3,2,1,0:T(8,128)S(1)} %pad_maximum_fusion.28), channel_id=1, source_target_pairs={{7,0},{0,1},{1,2},{2,3},{3,4},{4,5},{5,6},{6,7},{15,8},{8,9},{9,10... | collective-permute-start | bytes 215048 | tf_op jit(solution)/shard_map/ppermute | solution.py:32
  59.5 2.0 %copy-start.3 = (f32[7,2,5,256]{3,2,1,0:T(8,128)}, f32[7,2,5,256]{3,2,1,0:T(8,128)S(1)}, u32[]{:S(2)}) copy-start(f32[7,2,5,256]{3,2,1,0:T(8,128)S(1)} %collective-permute-done.2) | copy-start | bytes 215044
  59.5 5.9 %collective-permute-start.3 = (f32[7,2,5,256]{3,2,1,0:T(8,128)S(1)}, f32[7,2,5,256]{3,2,1,0:T(8,128)S(1)}, u32[]{:S(2)}, u32[]{:S(2)}) collective-permute-start(f32[7,2,5,256]{3,2,1,0:T(8,128)S(1)} %collective-permute-done.2), channel_id=1, source_target_pairs={{0,24},{8,0},{16,8},{24,16},{1,25},{9,1},{17,9},{25,17},{2,26},{10... | collective-permute-start | bytes 215048 | tf_op jit(solution)/shard_map/ppermute | solution.py:19
  65.5 8.9 %copy-start.9 = (f32[7,2,5,256]{3,2,1,0:T(8,128)}, f32[7,2,5,256]{3,2,1,0:T(8,128)S(1)}, u32[]{:S(2)}) copy-start(f32[7,2,5,256]{3,2,1,0:T(8,128)S(1)} %collective-permute-done.3) | copy-start | bytes 215044
  65.5 24.9 %copy-start.4 = (f32[7,2,5,256]{3,2,1,0:T(8,128)S(1)}, f32[7,2,5,256]{3,2,1,0:T(8,128)}, u32[]{:S(2)}) copy-start(f32[7,2,5,256]{3,2,1,0:T(8,128)} %copy-done.3) | copy-start | bytes 215044
  65.5 5.6 %collective-permute-start.4 = (f32[7,2,5,256]{3,2,1,0:T(8,128)S(1)}, f32[7,2,5,256]{3,2,1,0:T(8,128)S(1)}, u32[]{:S(2)}, u32[]{:S(2)}) collective-permute-start(f32[7,2,5,256]{3,2,1,0:T(8,128)S(1)} %collective-permute-done.3), channel_id=1, source_target_pairs={{0,24},{8,0},{16,8},{24,16},{1,25},{9,1},{17,9},{25,17},{2,26},{10... | collective-permute-start | bytes 215048 | tf_op jit(solution)/shard_map/ppermute | solution.py:19
  71.1 19.3 %collective-permute-start.5 = (f32[7,2,5,256]{3,2,1,0:T(8,128)S(1)}, f32[7,2,5,256]{3,2,1,0:T(8,128)S(1)}, u32[]{:S(2)}, u32[]{:S(2)}) collective-permute-start(f32[7,2,5,256]{3,2,1,0:T(8,128)S(1)} %collective-permute-done.4), channel_id=1, source_target_pairs={{0,24},{8,0},{16,8},{24,16},{1,25},{9,1},{17,9},{25,17},{2,26},{10... | collective-permute-start | bytes 215048 | tf_op jit(solution)/shard_map/ppermute | solution.py:19
  88.9 1.5 copy-start.10
  100.5 19.9 %collective-permute-start.11 = (f32[7,2,5,256]{3,1,2,0:T(2,128)S(1)}, f32[7,2,5,256]{3,1,2,0:T(2,128)S(1)}, u32[]{:S(2)}, u32[]{:S(2)}) collective-permute-start(f32[7,2,5,256]{3,1,2,0:T(2,128)S(1)} %pad_maximum_fusion.32), channel_id=1, source_target_pairs={{1,0},{2,1},{3,2},{4,3},{5,4},{6,5},{7,6},{0,7},{9,8},{10,9},{11,1... | collective-permute-start | bytes 215048 | tf_op jit(solution)/shard_map/ppermute | solution.py:32
  100.6 5.2 %collective-permute-start.7 = (f32[7,2,5,256]{3,2,1,0:T(8,128)S(1)}, f32[7,2,5,256]{3,2,1,0:T(8,128)S(1)}, u32[]{:S(2)}, u32[]{:S(2)}) collective-permute-start(f32[7,2,5,256]{3,2,1,0:T(8,128)S(1)} %pad_maximum_fusion.29), channel_id=1, source_target_pairs={{7,0},{0,1},{1,2},{2,3},{3,4},{4,5},{5,6},{6,7},{15,8},{8,9},{9,10... | collective-permute-start | bytes 215048 | tf_op jit(solution)/shard_map/ppermute | solution.py:32
  105.8 1.7 copy-start.5
  105.8 5.5 %collective-permute-start.8 = (f32[7,2,5,256]{3,2,1,0:T(8,128)S(1)}, f32[7,2,5,256]{3,2,1,0:T(8,128)S(1)}, u32[]{:S(2)}, u32[]{:S(2)}) collective-permute-start(f32[7,2,5,256]{3,2,1,0:T(8,128)S(1)} %collective-permute-done.7), channel_id=1, source_target_pairs={{0,24},{8,0},{16,8},{24,16},{1,25},{9,1},{17,9},{25,17},{2,26},{10... | collective-permute-start | bytes 215048 | tf_op jit(solution)/shard_map/ppermute | solution.py:19
  111.3 25.0 %copy-start.11 = (f32[7,2,5,256]{3,2,1,0:T(8,128)}, f32[7,2,5,256]{3,2,1,0:T(8,128)S(1)}, u32[]{:S(2)}) copy-start(f32[7,2,5,256]{3,2,1,0:T(8,128)S(1)} %collective-permute-done.8) | copy-start | bytes 215044
  111.3 25.2 %copy-start.6 = (f32[7,2,5,256]{3,2,1,0:T(8,128)S(1)}, f32[7,2,5,256]{3,2,1,0:T(8,128)}, u32[]{:S(2)}) copy-start(f32[7,2,5,256]{3,2,1,0:T(8,128)} %copy-done.5) | copy-start | bytes 215044
  111.3 5.9 %collective-permute-start.9 = (f32[7,2,5,256]{3,2,1,0:T(8,128)S(1)}, f32[7,2,5,256]{3,2,1,0:T(8,128)S(1)}, u32[]{:S(2)}, u32[]{:S(2)}) collective-permute-start(f32[7,2,5,256]{3,2,1,0:T(8,128)S(1)} %collective-permute-done.8), channel_id=1, source_target_pairs={{0,24},{8,0},{16,8},{24,16},{1,25},{9,1},{17,9},{25,17},{2,26},{10... | collective-permute-start | bytes 215048 | tf_op jit(solution)/shard_map/ppermute | solution.py:19
  117.1 19.3 %copy-start.12 = (f32[7,2,5,256]{3,2,1,0:T(8,128)}, f32[7,2,5,256]{3,2,1,0:T(8,128)S(1)}, u32[]{:S(2)}) copy-start(f32[7,2,5,256]{3,2,1,0:T(8,128)S(1)} %collective-permute-done.9) | copy-start | bytes 215044
  117.1 19.4 %collective-permute-start.10 = (f32[7,2,5,256]{3,2,1,0:T(8,128)S(1)}, f32[7,2,5,256]{3,2,1,0:T(8,128)S(1)}, u32[]{:S(2)}, u32[]{:S(2)}) collective-permute-start(f32[7,2,5,256]{3,2,1,0:T(8,128)S(1)} %collective-permute-done.9), channel_id=1, source_target_pairs={{0,24},{8,0},{16,8},{24,16},{1,25},{9,1},{17,9},{25,17},{2,26},{10... | collective-permute-start | bytes 215048 | tf_op jit(solution)/shard_map/ppermute | solution.py:19
  144.7 19.9 %collective-permute-start.16 = (f32[7,2,5,256]{3,1,2,0:T(2,128)S(1)}, f32[7,2,5,256]{3,1,2,0:T(2,128)S(1)}, u32[]{:S(2)}, u32[]{:S(2)}) collective-permute-start(f32[7,2,5,256]{3,1,2,0:T(2,128)S(1)} %pad_maximum_fusion.33), channel_id=1, source_target_pairs={{1,0},{2,1},{3,2},{4,3},{5,4},{6,5},{7,6},{0,7},{9,8},{10,9},{11,1... | collective-permute-start | bytes 215048 | tf_op jit(solution)/shard_map/ppermute | solution.py:32
  144.8 5.2 %collective-permute-start.12 = (f32[7,2,5,256]{3,2,1,0:T(8,128)S(1)}, f32[7,2,5,256]{3,2,1,0:T(8,128)S(1)}, u32[]{:S(2)}, u32[]{:S(2)}) collective-permute-start(f32[7,2,5,256]{3,2,1,0:T(8,128)S(1)} %pad_maximum_fusion.30), channel_id=1, source_target_pairs={{7,0},{0,1},{1,2},{2,3},{3,4},{4,5},{5,6},{6,7},{15,8},{8,9},{9,10... | collective-permute-start | bytes 215048 | tf_op jit(solution)/shard_map/ppermute | solution.py:32
  150.0 1.7 copy-start.1
  150.0 5.5 %collective-permute-start.13 = (f32[7,2,5,256]{3,2,1,0:T(8,128)S(1)}, f32[7,2,5,256]{3,2,1,0:T(8,128)S(1)}, u32[]{:S(2)}, u32[]{:S(2)}) collective-permute-start(f32[7,2,5,256]{3,2,1,0:T(8,128)S(1)} %collective-permute-done.12), channel_id=1, source_target_pairs={{0,24},{8,0},{16,8},{24,16},{1,25},{9,1},{17,9},{25,17},{2,26},{10... | collective-permute-start | bytes 215048 | tf_op jit(solution)/shard_map/ppermute | solution.py:19
  155.5 9.2 %copy-start.7 = (f32[7,2,5,256]{3,2,1,0:T(8,128)}, f32[7,2,5,256]{3,2,1,0:T(8,128)S(1)}, u32[]{:S(2)}) copy-start(f32[7,2,5,256]{3,2,1,0:T(8,128)S(1)} %collective-permute-done.13) | copy-start | bytes 215044
  155.5 25.4 %copy-start.2 = (f32[7,2,5,256]{3,2,1,0:T(8,128)S(1)}, f32[7,2,5,256]{3,2,1,0:T(8,128)}, u32[]{:S(2)}) copy-start(f32[7,2,5,256]{3,2,1,0:T(8,128)} %copy-done.1) | copy-start | bytes 215044
  155.5 5.8 %collective-permute-start.14 = (f32[7,2,5,256]{3,2,1,0:T(8,128)S(1)}, f32[7,2,5,256]{3,2,1,0:T(8,128)S(1)}, u32[]{:S(2)}, u32[]{:S(2)}) collective-permute-start(f32[7,2,5,256]{3,2,1,0:T(8,128)S(1)} %collective-permute-done.13), channel_id=1, source_target_pairs={{0,24},{8,0},{16,8},{24,16},{1,25},{9,1},{17,9},{25,17},{2,26},{10... | collective-permute-start | bytes 215048 | tf_op jit(solution)/shard_map/ppermute | solution.py:19
  161.3 19.6 %collective-permute-start.15 = (f32[7,2,5,256]{3,2,1,0:T(8,128)S(1)}, f32[7,2,5,256]{3,2,1,0:T(8,128)S(1)}, u32[]{:S(2)}, u32[]{:S(2)}) collective-permute-start(f32[7,2,5,256]{3,2,1,0:T(8,128)S(1)} %collective-permute-done.14), channel_id=1, source_target_pairs={{0,24},{8,0},{16,8},{24,16},{1,25},{9,1},{17,9},{25,17},{2,26},{10... | collective-permute-start | bytes 215048 | tf_op jit(solution)/shard_map/ppermute | solution.py:19
  179.4 1.5 copy-start.8
  186.1 0.6 copy-start.14
  186.1 0.6 copy-start.16
  186.1 0.7 copy-start.18
